TPU v7x, 128 devices: a whole 4x4x4 slice. The times are simulated.
128 devices in a mesh: blk: 16 (over z_lo, x, core), narrow: 8 (over z_hi, y).
Axes of the slice: x: 4, y: 4, z: 4 (z_hi: 2, z_lo: 2; z = z_hi * 2 + z_lo), core: 2. Of those that a mesh axis runs over, the one named last changes fastest.
Arguments:
- codes: bfloat16 [24576, 12288], P(('blk', 'narrow')), may hold values from -24 to 24
- signals: bfloat16 [24576, 192], P(('blk', 'narrow')), may hold values from -6 to 6
- dictionary: bfloat16 [12288, 192], P('blk'), may hold values from -0.0546875 to 0.0546875
Outputs:
- new_codes: bfloat16 [24576, 12288], P(('blk', 'narrow'))
- dict_grad: float32 [12288, 192], P(('blk', 'narrow'))
All inputs are finite; a program needn't handle non-finite values.
Results may differ from a plain program's by a relative error of at most 0.0095.
Values may be sent and summed in bfloat16 or wider, within the bound.
No kernel may reach another device: no remote copies, remote signals or barrier semaphores. Data moves between devices by JAX's collectives and lax.ppermute only.
A program may use at most 64 MiB of HBM per device.

v0:
```python
import jax
import jax.numpy as jnp
from jax import lax
from jax.sharding import PartitionSpec as P


def shrink(values):
    return jnp.sign(values) * jnp.maximum(jnp.abs(values) - 0.5, 0.0)


def body(codes, signals, dictionary):
    row_count = codes.shape[0]
    blk_size = lax.axis_size("blk")
    narrow_size = lax.axis_size("narrow")
    signal_float = signals.astype(jnp.float32)
    columns = codes
    estimate = jnp.dot(
        columns,
        lax.all_gather(dictionary, "blk", axis=0, tiled=True),
        preferred_element_type=jnp.float32,
    )
    misfit = (estimate - signal_float).astype(jnp.bfloat16)
    atoms_part = lax.all_gather(dictionary, "blk", axis=0, tiled=True)
    columns = codes
    correlation = lax.dot_general(
        misfit, atoms_part, (((1,), (1,)), ((), ())), preferred_element_type=jnp.float32
    )
    fresh_cols = shrink(columns.astype(jnp.float32) - 4.0 * correlation).astype(jnp.bfloat16)
    second = jnp.dot(fresh_cols, atoms_part, preferred_element_type=jnp.float32)
    misfit_two = (second - signal_float).astype(jnp.bfloat16)
    grad_scale = float(row_count * blk_size * narrow_size) ** (-0.5)
    columns = fresh_cols
    product = lax.dot_general(
        columns, misfit_two, (((0,), (0,)), ((), ())), preferred_element_type=jnp.float32
    )
    dict_grad = lax.psum_scatter(
        product * grad_scale, ("blk", "narrow"), scatter_dimension=0, tiled=True
    )
    return (fresh_cols, dict_grad)


def solution(mesh):
    placed = (P(("blk", "narrow"), None), P(("blk", "narrow"), None), P("blk", None))
    return jax.shard_map(
        body,
        mesh=mesh,
        in_specs=placed,
        out_specs=(P(("blk", "narrow"), None), P(("blk", "narrow"), None)),
        check_vma=False,
    )
```

profile of v0, /device:TPU:0, one launch (start us, length us, event | category | flops | bytes accessed | tf_op | source)
XLA Modules:
  0.0 752.3 jit_solution(6917375865547376117)
XLA Ops:
  7.2 0.0 all-gather.2.cloned.1.call-start
  7.2 0.7 all-gather.2.cloned.1.call-update
  7.9 0.0 copy-start.1
  7.9 0.0 reduce-scatter.2.cloned.1.call-start
  8.0 42.0 %all-gather.2.cloned.1.call-done = bf16[12288,192]{0,1:T(8,128)(2,1)} async-done(((bf16[768,192]{0,1:T(8,128)(2,1)}), bf16[12288,192]{0,1:T(8,128)(2,1)}) %all-gather.2.cloned.1.call-update) | async-done | bytes 4718608 | tf_op jit(solution)/shard_map/all_gather | solution.py:19
  50.0 16.0 %multiply_convert_fusion = bf16[192,12288]{1,0:T(8,128)(2,1)} fusion(bf16[12288,192]{0,1:T(8,128)(2,1)} %all-gather.2.cloned.1.call-done, bf16[192,12288]{1,0:T(8,128)(2,1)} %param.3, bf16[192,192]{1,0:T(8,128)(2,1)} %param.4), kind=kOutput, calls=%fused_computation.3 | convolution fusion | flops 1833283584 | bytes 14229504 | tf_op jit(solution)/shard_map/dot_general | solution.py:25
  66.0 0.0 copy-done.1
  66.0 0.0 copy-start
  66.0 5.3 fusion.2
  71.3 0.0 copy-done
  71.3 6.4 convolution_multiply_fusion
  77.8 0.0 reduce-scatter.2.cloned.1.call-update
  77.8 667.7 %reduce-scatter.2.cloned.1.call-done = f32[96,192]{1,0:T(8,128)} async-done(((f32[12288,192]{1,0:T(8,128)}), f32[96,192]{1,0:T(8,128)}) %reduce-scatter.2.cloned.1.call-update) | async-done | bytes 73744 | tf_op jit(solution)/shard_map/reduce_scatter | solution.py:36
Async XLA Ops:
  7.2 42.8 %all-gather.2.cloned.1.call-start = ((), (), s32[]{:S(2)}) async-start(), calls=%async_computation.1 | async-start | bytes 5013504 | tf_op jit(solution)/shard_map/all_gather | solution.py:19
  7.9 58.1 %copy-start.1 = (bf16[192,192]{1,0:T(8,128)(2,1)S(1)}, bf16[192,192]{1,0:T(8,128)(2,1)}, u32[]{:S(2)}) copy-start(bf16[192,192]{1,0:T(8,128)(2,1)} %param.4) | copy-start | bytes 221188
  7.9 737.5 %reduce-scatter.2.cloned.1.call-start = ((), (), s32[]{:S(2)}) async-start(), calls=%async_computation.2 | async-start | bytes 12681216 | tf_op jit(solution)/shard_map/reduce_scatter | solution.py:36
  66.0 5.3 copy-start
Sparse Core Ops, SparseCore 0:
  9.6 40.2 all-gather.1
  77.9 667.4 reduce-scatter.1
where the time goes:
time: 752 us
  waiting for transfers between devices  710 us (94%)
  matrix products  27.8 us (4%)
  between operations  14.1 us (2%)
    reduce_scatter x1, waiting for transfers between devices, body(): lax.psum_scatter(product * grad_scale, ('blk', 'narrow'), scatter_dimensi...  668 us
    all_gather x1, waiting for transfers between devices, body(): lax.all_gather(dictionary, 'blk', axis=0, tiled=True)  42 us
    dot_general x1, matrix products, body(): lax.dot_general(misfit, atoms_part, (((1,), (1,)), ((), ())), preferred_e...  16 us
  transfers between devices with their start and end apart: 2, of which 2 were waited for; matrix products, arithmetic and copies ran while one was open for 0% of the time, Pallas kernels for 0%

commit v1 on v0

--- a/solution.py
+++ b/solution.py
@@ -14,10 +14,17 @@
     narrow_size = lax.axis_size("narrow")
     signal_float = signals.astype(jnp.float32)
     columns = codes
+    packet_fill = lambda local_block, peer_axis: jnp.concatenate(
+        lax.all_to_all(
+            jnp.stack([local_block] * lax.psum(1, axis_name=peer_axis)),
+            axis_name=peer_axis,
+            split_axis=0,
+            concat_axis=0,
+        ),
+        axis=0,
+    )
     estimate = jnp.dot(
-        columns,
-        lax.all_gather(dictionary, "blk", axis=0, tiled=True),
-        preferred_element_type=jnp.float32,
+        columns, packet_fill(dictionary, peer_axis="blk"), preferred_element_type=jnp.float32
     )
     misfit = (estimate - signal_float).astype(jnp.bfloat16)
     atoms_part = lax.all_gather(dictionary, "blk", axis=0, tiled=True)

time: 752 us -> 798 us (1.061)
  blocking collectives: 0 us -> 79.5 us
  waiting for transfers between devices: 710 us -> 672 us
    all_to_all x0 -> x1, blocking collectives: none -> 79.5 us  [body(): lax.all_to_all(jnp.stack([local_block] * lax.psum(1, axis_name=peer_axis)...]
    all_gather x1, waiting for transfers between devices: 42 us -> 1.42 us  [body(): atoms_part = lax.all_gather(dictionary, 'blk', axis=0, tiled=True)]
  transfers between devices with their start and end apart: 2 -> 2, of which waited for: 2 -> 2; matrix products, arithmetic and copies ran while one was open for 0% -> 1% of each run, Pallas kernels for 0% -> 0%
where the time goes in v1:
time: 798 us; the launch traced here: 797 us
  waiting for transfers between devices  672 us (84%)
  blocking collectives  79.5 us (10%)
  matrix products  27.8 us (3%)
  between operations  14.1 us (2%)
    reduce_scatter x1, waiting for transfers between devices, body(): lax.psum_scatter(product * grad_scale, ('blk', 'narrow'), scatter_dimensi...  670 us
    all_to_all x1, blocking collectives, body(): lax.all_to_all(jnp.stack([local_block] * lax.psum(1, axis_name=peer_axis)...  79.5 us
    dot_general x1, matrix products, body(): lax.dot_general(misfit, atoms_part, (((1,), (1,)), ((), ())), preferred_e...  16 us
  transfers between devices with their start and end apart: 2, of which 2 were waited for; matrix products, arithmetic and copies ran while one was open for 1% of the time, Pallas kernels for 0%

profile of v1, /device:TPU:0, one launch (start us, length us, event | category | flops | bytes accessed | tf_op | source)
XLA Modules:
  0.0 797.5 jit_solution(8642645024768589274)
XLA Ops:
  7.2 0.0 all-gather.2.cloned.1.call-start
  7.2 0.7 all-gather.2.cloned.1.call-update
  7.9 0.0 reduce-scatter.2.cloned.1.call-start
  7.9 1.4 stack.2
  9.4 79.5 %all_to_all.5 = bf16[16,768,192]{1,2,0:T(8,128)(2,1)S(1)} all-to-all(bf16[16,768,192]{1,2,0:T(8,128)(2,1)S(1)} %stack.2), channel_id=1, replica_groups=mesh['blk'=16,'narrow'=8] {'blk'}, dimensions={0} | all-to-all | bytes 9437184 | tf_op jit(solution)/shard_map/all_to_all | solution.py:18
  88.9 0.0 copy-start.1
  88.9 2.7 copy.7
  91.6 1.4 all-gather.2.cloned.1.call-done
  93.0 0.0 copy-done.1
  93.0 16.0 %multiply_convert_fusion = bf16[192,12288]{1,0:T(8,128)(2,1)} fusion(bf16[12288,192]{0,1:T(8,128)(2,1)} %all-gather.2.cloned.1.call-done, bf16[192,12288]{1,0:T(8,128)(2,1)} %param.3, bf16[12288,192]{0,1:T(8,128)(2,1)} %bitcast.10, bf16[192,192]{1,0:T(8,128)(2,1)S(1)} %copy-done.1), kind=kOutput, calls=%fused_computation.3 | convolution fusion | flops 1833283584 | bytes 18948096 | tf_op jit(solution)/shard_map/dot_general | solution.py:32
  109.0 0.0 copy-start
  109.0 5.3 fusion.2
  114.4 0.0 copy-done
  114.4 6.4 convolution_multiply_fusion
  120.8 0.0 reduce-scatter.2.cloned.1.call-update
  120.8 669.8 %reduce-scatter.2.cloned.1.call-done = f32[96,192]{1,0:T(8,128)} async-done(((f32[12288,192]{1,0:T(8,128)}), f32[96,192]{1,0:T(8,128)}) %reduce-scatter.2.cloned.1.call-update) | async-done | bytes 73744 | tf_op jit(solution)/shard_map/reduce_scatter | solution.py:43
Async XLA Ops:
  7.2 85.9 %all-gather.2.cloned.1.call-start = ((), (), s32[]{:S(2)}) async-start(), calls=%async_computation.2 | async-start | bytes 5013504 | tf_op jit(solution)/shard_map/all_gather | solution.py:30
  7.9 782.8 %reduce-scatter.2.cloned.1.call-start = ((), (), s32[]{:S(2)}) async-start(), calls=%async_computation.3 | async-start | bytes 12681216 | tf_op jit(solution)/shard_map/reduce_scatter | solution.py:43
  88.9 4.1 copy-start.1
  109.0 5.3 copy-start
Sparse Core Ops, SparseCore 0:
  9.6 83.3 all-gather.1
  120.9 669.6 reduce-scatter.1
